TPU v7x, 32 devices: a whole 2x2x4 slice. The times are simulated.
32 devices in a mesh: scene: 2 (over y), tok: 4 (over z), col: 2 (over x), rep: 2 (over core).
Axes of the slice: x: 2, y: 2, z: 4, core: 2. Of those that a mesh axis runs over, the one named last changes fastest.
Arguments:
- tokens: float32 [8192, 512], P(('scene', 'tok'), ('col', 'rep')), parts along dimension 0
- w_qkv: float32 [2, 3, 512, 512], P(None, None, None, ('col', 'rep'))
- w_out: float32 [2, 512, 512], P(None, ('col', 'rep')), may hold values from -0.25 to 0.25
- w_up: float32 [2, 512, 2048], P(None, None, ('col', 'rep')), may hold values from -0.25 to 0.25
- w_down: float32 [2, 2048, 512], P(None, ('col', 'rep')), may hold values from -0.125 to 0.125
- attn_gain: float32 [2, 512], replicated, may hold values from 0.1 to 1.9
- mlp_gain: float32 [2, 512], replicated, may hold values from 0.1 to 1.9
- dest_device: int32 [128], P(('scene', 'tok')), parts along dimension 0, may hold values from 0 to 3, as said below
- dest_slot: int32 [128], P(('scene', 'tok')), parts along dimension 0, may hold values from 0 to 15, as said below
- pillar: int32 [8192], P(('scene', 'tok')), parts along dimension 0, may hold values from -1 to 2047, as said below
- depth_weight: float32 [2, 3, 3, 512], replicated, may hold values from -2 to 2
- point_weight: float32 [2, 512, 1024], replicated, may hold values from -0.25 to 0.25
- raster_gain: float32 [2, 512], replicated, may hold values from 0.1 to 1.9
Outputs:
- raster: float32 [128, 32, 512], P(('scene', 'tok', 'rep'), 'col'), parts along dimension 0
There are 2 independent parts, one for each index of `scene`. A program takes and returns all parts, laid end to end along the dimension named above; an argument that names none is the same for every part. Nothing has to cross between parts.
Inputs may be any that keep to these rules, and one draw needn't show every extreme that they name: `dest_device`: together with dest_slot the blocks fill every index of tok's 16 slots exactly once. At most 5 blocks of one index of tok go to one index, and every index sends exactly 5 blocks to some index. `dest_slot`: the slot of the block among the 16 of its destination. The token at Hilbert position t has a cell in raster rows i * 16 to (i + 1) * 16 - 1 with i = t // 1024, or -1 if it has no pillar; several tokens may share a cell.
All inputs are finite; a program needn't handle non-finite values.
Results may differ from a plain program's by a relative error of at most 0.00012.
Values sent between devices are 32-bit elements; how exact they have to be, the bound alone decides.
A program may use at most 128 MiB of HBM per device.

v0:
```python
import jax
import jax.numpy as jnp
from jax import lax
from jax.sharding import PartitionSpec as P

PATCH = 1024
TR = 16
TC = 16
HD = 16
MATMUL_PRECISION = lax.Precision.HIGHEST
EPSILON = 1e-05


def padded(block, sides, width):
    for axis, dim in sides:
        count = lax.axis_size(axis)
        forward = [(i, i + 1) for i in range(count - 1)]
        backward = [(target, source) for source, target in forward]
        low = lax.ppermute(
            lax.slice_in_dim(block, block.shape[dim] - width, None, axis=dim), axis, forward
        )
        high = lax.ppermute(lax.slice_in_dim(block, 0, width, axis=dim), axis, backward)
        block = jnp.concatenate([low, block, high], axis=dim)
    return block


def layer_norm(values, gain_row):
    average = jnp.mean(values, axis=-1, keepdims=True)
    centered = values - average
    variance = jnp.mean(centered * centered, axis=-1, keepdims=True)
    return centered * lax.rsqrt(variance + EPSILON) * gain_row


def patch_attention(query_projection, key_proj, value_proj):
    scores = jnp.einsum(
        "qhd,khd->hqk", query_projection, key_proj, precision=MATMUL_PRECISION
    ) * HD ** (-0.5)
    scores = scores - jnp.max(scores, axis=-1, keepdims=True)
    weights = jnp.exp(scores)
    weights = weights / jnp.sum(weights, axis=-1, keepdims=True)
    return jnp.einsum("hqk,khd->qhd", weights, value_proj, precision=MATMUL_PRECISION)


def matmul(left, right):
    return jnp.dot(left, right, precision=MATMUL_PRECISION, preferred_element_type=jnp.float32)


def widen(slice_cols):
    return lax.all_gather(slice_cols, ("col", "rep"), axis=1, tiled=True)


def block_layer(stream, layer_index, w_qkv, w_out, w_up, w_down, attn_gain, mlp_gain):
    row_count = stream.shape[0]
    local_cols = w_qkv.shape[-1]
    heads_here = local_cols // HD
    normed = layer_norm(stream, attn_gain[layer_index])
    shaped = tuple(
        (
            matmul(normed, w_qkv[layer_index, j]).reshape(row_count // PATCH, PATCH, heads_here, HD)
            for j in range(3)
        )
    )

    def attend_patch(operands):
        return patch_attention(operands[0], operands[1], operands[2]).reshape(PATCH, local_cols)

    attended = lax.map(attend_patch, shaped).reshape(row_count, local_cols)
    partial_out = matmul(attended, w_out[layer_index])
    stream = stream + lax.psum(partial_out, ("col", "rep"))
    normed = layer_norm(stream, mlp_gain[layer_index])
    hidden = jax.nn.gelu(matmul(normed, w_up[layer_index]), approximate=False)
    partial_mlp = matmul(hidden, w_down[layer_index])
    summed_share = lax.psum_scatter(partial_mlp, ("col", "rep"), scatter_dimension=1, tiled=True)
    feature_width = summed_share.shape[1]
    own_cols = lax.dynamic_slice_in_dim(
        stream, lax.axis_index(("col", "rep")) * feature_width, feature_width, 1
    )
    return own_cols + summed_share


def send_blocks(block_list, dest_device, dest_slot):
    block_count, rows_per_block, feature_width = block_list.shape
    peers = lax.axis_size("tok")
    capacity = max(2, (block_count + peers - 4) // (peers - 1))
    order_index = jnp.arange(block_count, dtype=jnp.int32)
    earlier = (dest_device[:, None] == dest_device[None, :]) & (
        order_index[None, :] < order_index[:, None]
    )
    prior_count = jnp.sum(earlier.astype(jnp.int32), axis=1)
    slot_key = dest_device * capacity + prior_count
    select_entries = (
        jnp.arange(peers * capacity, dtype=jnp.int32)[:, None] == slot_key[None, :]
    ).astype(jnp.float32)
    outgoing = jnp.einsum(
        "jb,brf->jrf", select_entries, block_list, precision=MATMUL_PRECISION
    ).reshape(peers, capacity, rows_per_block, feature_width)
    slot_codes = matmul(select_entries, (dest_slot + 1).astype(jnp.float32)).reshape(
        peers, capacity
    )
    incoming, arrived = (
        lax.all_to_all(outgoing, "tok", split_axis=0, concat_axis=0, tiled=True),
        lax.all_to_all(slot_codes, "tok", split_axis=0, concat_axis=0, tiled=True),
    )
    wanted = (order_index + 1).astype(jnp.float32)
    placing = (wanted[:, None] == arrived.reshape(-1)[None, :]).astype(jnp.float32)
    flat_incoming = incoming.reshape(peers * capacity, rows_per_block, feature_width)
    return jnp.einsum("sj,jrf->srf", placing, flat_incoming, precision=MATMUL_PRECISION)


def raster_cells(extended, depth_weight, point_weight, gain_row):
    row_count = extended.shape[0] - 2
    col_count = extended.shape[1] - 2
    count_of_channels = extended.shape[2]
    normed = (
        extended
        * lax.rsqrt(jnp.mean(extended * extended, axis=-1, keepdims=True) + EPSILON)
        * gain_row
    )
    mixed_cells = jnp.zeros((row_count, col_count, count_of_channels), jnp.float32)
    for row_tap in range(3):
        for col_tap in range(3):
            mixed_cells = (
                mixed_cells
                + normed[row_tap : row_tap + row_count, col_tap : col_tap + col_count]
                * depth_weight[row_tap, col_tap]
            )
    combined = matmul(mixed_cells.reshape(row_count * col_count, count_of_channels), point_weight)
    combined = combined.reshape(row_count, col_count, 2 * count_of_channels)
    centre = extended[1:-1, 1:-1]
    return centre + combined[..., :count_of_channels] * jax.nn.sigmoid(
        combined[..., count_of_channels:]
    )


def on_device(
    tokens,
    w_qkv,
    w_out,
    w_up,
    w_down,
    attn_gain,
    mlp_gain,
    dest_device,
    dest_slot,
    pillar,
    depth_weight,
    point_weight,
    raster_gain,
):
    stream = widen(tokens)
    first_out = block_layer(stream, 0, w_qkv, w_out, w_up, w_down, attn_gain, mlp_gain)
    feature_width = first_out.shape[1]
    block_count = dest_device.shape[0]
    block_list = first_out.reshape(block_count, first_out.shape[0] // block_count, feature_width)
    reordered_tokens = send_blocks(block_list, dest_device, dest_slot)
    stream = widen(reordered_tokens.reshape(-1, feature_width))
    stream = widen(block_layer(stream, 1, w_qkv, w_out, w_up, w_down, attn_gain, mlp_gain))
    rep_rows = TR // lax.axis_size("rep")
    row_start = lax.axis_index(("tok", "rep")) * rep_rows
    col_start = lax.axis_index("col") * TC
    full_width = TC * lax.axis_size("col")
    cell_rows = row_start + jnp.arange(rep_rows, dtype=jnp.int32)[:, None]
    cell_ids = (
        cell_rows * full_width + col_start + jnp.arange(TC, dtype=jnp.int32)[None, :]
    ).reshape(-1)
    onehot = (pillar[:, None] == cell_ids[None, :]).astype(jnp.float32)
    raster = jnp.einsum("tc,td->cd", onehot, stream, precision=MATMUL_PRECISION).reshape(
        rep_rows, TC, -1
    )
    for layer_index in range(2):
        extended = padded(raster, ((("tok", "rep"), 0), ("col", 1)), 1)
        raster = raster_cells(
            extended, depth_weight[layer_index], point_weight[layer_index], raster_gain[layer_index]
        )
    return raster


def solution(mesh):
    placed = (
        P(("scene", "tok"), ("col", "rep")),
        P(None, None, None, ("col", "rep")),
        P(None, ("col", "rep"), None),
        P(None, None, ("col", "rep")),
        P(None, ("col", "rep"), None),
        P(),
        P(),
        P(("scene", "tok")),
        P(("scene", "tok")),
        P(("scene", "tok")),
        P(),
        P(),
        P(),
    )
    return jax.shard_map(
        on_device,
        mesh=mesh,
        in_specs=placed,
        out_specs=P(("scene", "tok", "rep"), "col", None),
        check_vma=False,
    )
```

profile of v0, /device:TPU:1, one launch (start us, length us, event | category | flops | bytes accessed | tf_op | source)
XLA Modules:
  0.0 510.4 jit_solution(3229951573968464027)
XLA Ops:
  9.9 24.3 %all-gather.4.cloned.1.call-done = f32[1024,512]{1,0:T(8,128)} async-done(((f32[1024,128]{1,0:T(8,128)}), f32[1024,512]{1,0:T(8,128)}) %all-gather.4.cloned.1.call-update) | async-done | bytes 2097168 | tf_op jit(solution)/shard_map/all_gather | solution.py:49
  42.0 28.0 %multiply_reduce_fusion.1 = (f32[8,1024]{1,0:T(8,128)S(1)}, f32[8,1024,1024]{1,2,0:T(8,128)S(1)}) fusion(f32[1024,8,16]{0,2,1:T(8,128)S(1)} %fusion.32, f32[1024,8,16]{0,2,1:T(8,128)S(1)} %fusion.30), kind=kOutput, calls=%fused_computation.7 | convolution fusion | flops 1627381760 | bytes 34635776 | tf_op jit(solution)/shard_map/while/body/eval_jaxpr/qhd,khd->hqk/dot_general | solution.py:35
  70.0 5.9 %fusion.4 = f32[8,1024]{1,0:T(8,128)S(1)} fusion(f32[8,1024,1024]{1,2,0:T(8,128)S(1)} %get-tuple-element.80, f32[8,1024]{1,0:T(8,128)S(1)} %get-tuple-element.79), kind=kLoop, calls=%fused_computation.8 | loop fusion | flops 25157632 | bytes 33619968 | tf_op jit(solution)/shard_map/while/body/eval_jaxpr/reduce_sum | solution.py:40
  75.9 5.2 %copy-done = f32[8,1024,1024]{1,2,0:T(8,128)} copy-done((f32[8,1024,1024]{1,2,0:T(8,128)}, f32[8,1024,1024]{1,2,0:T(8,128)S(1)}, u32[]{:S(2)}) %copy-start) | copy-done | bytes 33554456
  84.4 25.6 %fusion.2 = f32[8,16,1024]{2,1,0:T(8,128)S(1)} fusion(f32[1024,8,16]{0,2,1:T(8,128)} %fusion.34, f32[8,1024,1024]{1,2,0:T(8,128)} %copy-done, f32[8,1024]{1,0:T(8,128)S(1)} %fusion.4, f32[8,1024]{1,0:T(8,128)S(1)} %get-tuple-element.79), kind=kOutput, calls=%fused_computation.4 | convolution fusion | flops 1635778560 | bytes 34668544 | tf_op jit(solution)/shard_map/while/body/eval_jaxpr/hqk,khd->qhd/dot_general | solution.py:41
  110.0 4.1 fusion.299
  114.3 50.8 %all-reduce.3.cloned.1.call-done = f32[1024,512]{1,0:T(8,128)} async-done(((f32[1024,512]{1,0:T(8,128)}), f32[1024,512]{1,0:T(8,128)}) %all-reduce.3.cloned.1.call-update) | async-done | bytes 2097168 | tf_op jit(solution)/shard_map/psum | solution.py:69
  169.3 3.7 fusion.143
  173.0 9.5 %fusion.14 = f32[1024,512]{1,0:T(8,128)} fusion(f32[1024,512]{1,0:T(8,128)S(1)} %fusion.143, f32[2,512,512]{2,1,0:T(8,128)S(1)} %copy-done.15), kind=kOutput, calls=%fused_computation.20 | convolution fusion | flops 3254779904 | bytes 5242880 | tf_op jit(solution)/shard_map/dot_general | solution.py:45
  184.1 4.3 all-to-all-start
  188.5 25.5 %reduce-scatter.3.cloned.1.call-done = f32[1024,128]{1,0:T(8,128)} async-done(((f32[1024,512]{1,0:T(8,128)}), f32[1024,128]{1,0:T(8,128)}) %reduce-scatter.3.cloned.1.call-update) | async-done | bytes 524304 | tf_op jit(solution)/shard_map/reduce_scatter | solution.py:73
  217.1 4.3 all-to-all-start.1
  222.7 15.6 %all-to-all-done.1 = f32[4,5,64,128]{3,2,1,0:T(8,128)S(1)} async-done(((f32[4,5,64,128]{3,2,1,0:T(8,128)}), f32[4,5,64,128]{3,2,1,0:T(8,128)S(1)}, u32[]{:S(2)}, u32[]{:S(2)}) %all-to-all-start.1) | async-done | bytes 655392 | tf_op jit(solution)/shard_map/all_to_all | solution.py:101
  240.6 21.8 %all-gather.6.cloned.1.call-done = f32[1024,512]{1,0:T(8,128)} async-done(((f32[1024,128]{1,0:T(8,128)}), f32[1024,512]{1,0:T(8,128)}) %all-gather.6.cloned.1.call-update) | async-done | bytes 2097168 | tf_op jit(solution)/shard_map/all_gather | solution.py:49
  270.1 27.9 %multiply_reduce_fusion = (f32[8,1024]{1,0:T(8,128)S(1)}, f32[8,1024,1024]{1,2,0:T(8,128)S(1)}) fusion(f32[1024,8,16]{0,2,1:T(8,128)S(1)} %fusion.26, f32[1024,8,16]{0,2,1:T(8,128)S(1)} %fusion.24), kind=kOutput, calls=%fused_computation.6 | convolution fusion | flops 1627381760 | bytes 34635776 | tf_op jit(solution)/shard_map/while/body/eval_jaxpr/qhd,khd->hqk/dot_general | solution.py:35
  298.0 5.9 %fusion.5 = f32[8,1024]{1,0:T(8,128)S(1)} fusion(f32[8,1024,1024]{1,2,0:T(8,128)S(1)} %get-tuple-element.82, f32[8,1024]{1,0:T(8,128)S(1)} %get-tuple-element.81), kind=kLoop, calls=%fused_computation.9 | loop fusion | flops 25157632 | bytes 33619968 | tf_op jit(solution)/shard_map/while/body/eval_jaxpr/reduce_sum | solution.py:40
  303.9 5.2 %copy-done.1 = f32[8,1024,1024]{1,2,0:T(8,128)} copy-done((f32[8,1024,1024]{1,2,0:T(8,128)}, f32[8,1024,1024]{1,2,0:T(8,128)S(1)}, u32[]{:S(2)}) %copy-start.1) | copy-done | bytes 33554456
  311.7 25.0 %fusion = f32[8,16,1024]{2,1,0:T(8,128)S(1)} fusion(f32[1024,8,16]{0,2,1:T(8,128)S(1)} %fusion.28, f32[8,1024,1024]{1,2,0:T(8,128)} %copy-done.1, f32[8,1024]{1,0:T(8,128)S(1)} %fusion.5, f32[8,1024]{1,0:T(8,128)S(1)} %get-tuple-element.81), kind=kOutput, calls=%fused_computation.2 | convolution fusion | flops 1635778560 | bytes 34668544 | tf_op jit(solution)/shard_map/while/body/eval_jaxpr/hqk,khd->qhd/dot_general | solution.py:41
  336.7 4.1 fusion.297
  340.8 50.8 %all-reduce.5.cloned.1.call-done = f32[1024,512]{1,0:T(8,128)} async-done(((f32[1024,512]{1,0:T(8,128)}), f32[1024,512]{1,0:T(8,128)}) %all-reduce.5.cloned.1.call-update) | async-done | bytes 2097168 | tf_op jit(solution)/shard_map/psum | solution.py:69
  395.9 3.7 fusion.89
  399.6 9.5 %fusion.18 = f32[1024,512]{1,0:T(8,128)} fusion(f32[1024,512]{1,0:T(8,128)S(1)} %fusion.89, f32[2,512,512]{2,1,0:T(8,128)S(1)} %copy-done.16), kind=kOutput, calls=%fused_computation.23 | convolution fusion | flops 3254779904 | bytes 5242880 | tf_op jit(solution)/shard_map/dot_general | solution.py:45
  409.2 31.4 %reduce-scatter.5.cloned.1.call-done = f32[1024,128]{1,0:T(8,128)} async-done(((f32[1024,512]{1,0:T(8,128)}), f32[1024,128]{1,0:T(8,128)}) %reduce-scatter.5.cloned.1.call-update) | async-done | bytes 524304 | tf_op jit(solution)/shard_map/reduce_scatter | solution.py:73
  442.9 23.3 %all-gather.8.cloned.1.call-done = f32[1024,512]{1,0:T(8,128)} async-done(((f32[1024,128]{1,0:T(8,128)}), f32[1024,512]{1,0:T(8,128)}) %all-gather.8.cloned.1.call-update) | async-done | bytes 2097168 | tf_op jit(solution)/shard_map/all_gather | solution.py:49
  (136 shorter events, 80.7 us)
Async XLA Ops:
  6.5 27.7 %all-gather.4.cloned.1.call-start = ((), (), s32[]{:S(2)}) async-start(), calls=%async_computation.4 | async-start | bytes 2621440 | tf_op jit(solution)/shard_map/all_gather | solution.py:49
  7.3 157.8 %all-reduce.3.cloned.1.call-start = ((), (), s32[]{:S(2)}) async-start(), calls=%async_computation.5 | async-start | bytes 4194304 | tf_op jit(solution)/shard_map/psum | solution.py:69
  70.0 11.1 %copy-start = (f32[8,1024,1024]{1,2,0:T(8,128)}, f32[8,1024,1024]{1,2,0:T(8,128)S(1)}, u32[]{:S(2)}) copy-start(f32[8,1024,1024]{1,2,0:T(8,128)S(1)} %get-tuple-element.80) | copy-start | bytes 100663296
  114.2 99.8 %reduce-scatter.3.cloned.1.call-start = ((), (), s32[]{:S(2)}) async-start(), calls=%async_computation.6 | async-start | bytes 2621440 | tf_op jit(solution)/shard_map/reduce_scatter | solution.py:73
  184.1 33.0 %all-to-all-start = ((f32[4,1,5]{2,1,0:T(1,128)}), f32[4,1,5]{2,1,0:T(1,128)S(1)}, u32[]{:S(2)}, u32[]{:S(2)}) async-start(f32[4,1,5]{2,1,0:T(1,128)} %bitcast.2), calls=%async_computation | async-start | bytes 4096 | tf_op jit(solution)/shard_map/all_to_all | solution.py:102
  217.1 21.2 %all-to-all-start.1 = ((f32[4,5,64,128]{3,2,1,0:T(8,128)}), f32[4,5,64,128]{3,2,1,0:T(8,128)S(1)}, u32[]{:S(2)}, u32[]{:S(2)}) async-start(f32[4,5,64,128]{3,2,1,0:T(8,128)} %copy.48), calls=%async_computation.2 | async-start | bytes 1310720 | tf_op jit(solution)/shard_map/all_to_all | solution.py:101
  221.5 40.9 %all-gather.6.cloned.1.call-start = ((), (), s32[]{:S(2)}) async-start(), calls=%async_computation.7 | async-start | bytes 2621440 | tf_op jit(solution)/shard_map/all_gather | solution.py:49
  240.1 151.6 %all-reduce.5.cloned.1.call-start = ((), (), s32[]{:S(2)}) async-start(), calls=%async_computation.8 | async-start | bytes 4194304 | tf_op jit(solution)/shard_map/psum | solution.py:69
  298.0 11.1 %copy-start.1 = (f32[8,1024,1024]{1,2,0:T(8,128)}, f32[8,1024,1024]{1,2,0:T(8,128)S(1)}, u32[]{:S(2)}) copy-start(f32[8,1024,1024]{1,2,0:T(8,128)S(1)} %get-tuple-element.82) | copy-start | bytes 100663296
  340.8 99.8 %reduce-scatter.5.cloned.1.call-start = ((), (), s32[]{:S(2)}) async-start(), calls=%async_computation.9 | async-start | bytes 2621440 | tf_op jit(solution)/shard_map/reduce_scatter | solution.py:73
  393.6 6.0 %copy-start.5 = (f32[1024,512]{1,0:T(8,128)}, f32[1024,512]{1,0:T(8,128)S(1)}, u32[]{:S(2)}) copy-start(f32[1024,512]{1,0:T(8,128)S(1)} %get-tuple-element.24) | copy-start | bytes 6291460
  409.1 33.7 %copy-start.9 = (f32[2,3,3,512]{3,0,2,1:T(2,128)S(1)}, f32[2,3,3,512]{3,0,2,1:T(2,128)}, u32[]{:S(2)}) copy-start(f32[2,3,3,512]{3,0,2,1:T(2,128)} %param.23) | copy-start | bytes 110596
  409.1 57.1 %copy-start.13 = (s32[1024]{0:T(1024)S(1)}, s32[1024]{0:T(1024)}, u32[]{:S(2)}) copy-start(s32[1024]{0:T(1024)} %param.22) | copy-start | bytes 12292
  409.1 57.1 %all-gather.8.cloned.1.call-start = ((), (), s32[]{:S(2)}) async-start(), calls=%async_computation.10 | async-start | bytes 2621440 | tf_op jit(solution)/shard_map/all_gather | solution.py:49
  442.7 38.5 %copy-start.12 = (f32[2,512]{1,0:T(2,128)S(1)}, f32[2,512]{1,0:T(2,128)}, u32[]{:S(2)}) copy-start(f32[2,512]{1,0:T(2,128)} %param.25) | copy-start | bytes 12292
  466.3 18.4 %copy-start.14 = (f32[2,512,1024]{2,1,0:T(8,128)S(1)}, f32[2,512,1024]{2,1,0:T(8,128)}, u32[]{:S(2)}) copy-start(f32[2,512,1024]{2,1,0:T(8,128)} %param.24) | copy-start | bytes 12582916
  469.1 5.2 %collective-permute-start = (f32[1,16,512]{2,1,0:T(8,128)S(1)}, f32[1,16,512]{2,1,0:T(8,128)S(1)}, u32[]{:S(2)}, u32[]{:S(2)}) collective-permute-start(f32[1,16,512]{2,1,0:T(8,128)S(1)} %get-tuple-element.51), channel_id=1, source_target_pairs={{0,1},{1,4},{4,5},{5,8},{8,9},{9,12},{12,13},{2,3},{3,6},{6,7},{7,... | collective-permute-start | bytes 98312 | tf_op jit(solution)/shard_map/ppermute | solution.py:19
  472.4 5.2 %collective-permute-start.1 = (f32[1,16,512]{2,1,0:T(8,128)S(1)}, f32[1,16,512]{2,1,0:T(8,128)S(1)}, u32[]{:S(2)}, u32[]{:S(2)}) collective-permute-start(f32[1,16,512]{2,1,0:T(8,128)S(1)} %get-tuple-element.52), channel_id=1, source_target_pairs={{1,0},{4,1},{5,4},{8,5},{9,8},{12,9},{13,12},{3,2},{6,3},{7,6},{10... | collective-permute-start | bytes 98312 | tf_op jit(solution)/shard_map/ppermute | solution.py:22
  477.6 3.5 collective-permute-start.2
  479.8 4.5 collective-permute-start.3
  486.2 5.3 %collective-permute-start.4 = (f32[1,16,512]{2,1,0:T(8,128)S(1)}, f32[1,16,512]{2,1,0:T(8,128)S(1)}, u32[]{:S(2)}, u32[]{:S(2)}) collective-permute-start(f32[1,16,512]{2,1,0:T(8,128)S(1)} %get-tuple-element.49), channel_id=1, source_target_pairs={{0,1},{1,4},{4,5},{5,8},{8,9},{9,12},{12,13},{2,3},{3,6},{6,7},{7,... | collective-permute-start | bytes 98312 | tf_op jit(solution)/shard_map/ppermute | solution.py:19
  489.6 5.2 %collective-permute-start.5 = (f32[1,16,512]{2,1,0:T(8,128)S(1)}, f32[1,16,512]{2,1,0:T(8,128)S(1)}, u32[]{:S(2)}, u32[]{:S(2)}) collective-permute-start(f32[1,16,512]{2,1,0:T(8,128)S(1)} %get-tuple-element.50), channel_id=1, source_target_pairs={{1,0},{4,1},{5,4},{8,5},{9,8},{12,9},{13,12},{3,2},{6,3},{7,6},{10... | collective-permute-start | bytes 98312 | tf_op jit(solution)/shard_map/ppermute | solution.py:22
  494.9 2.7 collective-permute-start.6
  496.2 4.5 collective-permute-start.7
  (12 other events, 33.8 us)
Sparse Core Ops, SparseCore 0:
  8.9 25.2 all-gather.3
  114.3 50.7 all-reduce.2
  182.6 31.3 reduce-scatter.2
  240.2 22.0 all-gather.5
  340.9 50.7 all-reduce.4
  409.3 31.2 reduce-scatter.4
  442.8 23.4 all-gather.7
where the time goes:
time: 515 us; the launch traced here: 510 us
  waiting for transfers between devices  257 us (50%)
  matrix products  165 us (32%)
  other arithmetic  27 us (5%)
  starting transfers between devices  25.4 us (5%)
  local copies, waits for them, and re-layouts  21.6 us (4%)
  between operations  14.3 us (3%)
    psum x2, waiting for transfers between devices, block_layer(): stream = stream + lax.psum(partial_out, ('col', 'rep'))  102 us
    all_gather x3, waiting for transfers between devices, widen(): return lax.all_gather(slice_cols, ('col', 'rep'), axis=1, tiled=True)  69.4 us
    reduce_scatter x2, waiting for transfers between devices, block_layer(): lax.psum_scatter(partial_mlp, ('col', 'rep'), scatter_dimension=1, tiled=...  56.9 us
    dot_general x2, matrix products, patch_attention(): jnp.einsum('qhd,khd->hqk', query_projection, key_proj, precision=MATMUL_P...  56 us
    dot_general x15, matrix products, matmul(): jnp.dot(left, right, precision=MATMUL_PRECISION, preferred_element_type=j...  53.7 us
    dot_general x2, matrix products, patch_attention(): jnp.einsum('hqk,khd->qhd', weights, value_proj, precision=MATMUL_PRECISION)  50.6 us
    unnamed x45, local copies, waits for them, and re-layouts  16.8 us
    all_to_all x1, waiting for transfers between devices, send_blocks(): lax.all_to_all(outgoing, 'tok', split_axis=0, concat_axis=0, tiled=True)  15.6 us
  transfers between devices with their start and end apart: 17, of which 12 were waited for; matrix products, arithmetic and copies ran while one was open for 2% of the time, Pallas kernels for 0%

commit v1 on v0

--- a/solution.py
+++ b/solution.py
@@ -66,7 +66,11 @@
 
     attended = lax.map(attend_patch, shaped).reshape(row_count, local_cols)
     partial_out = matmul(attended, w_out[layer_index])
-    stream = stream + lax.psum(partial_out, ("col", "rep"))
+
+    def save_shapes(x_part, row_axis):
+        return lax.all_gather(x_part, axis_name=row_axis).sum(axis=0)
+
+    stream = stream + save_shapes(partial_out, ("col", "rep"))
     normed = layer_norm(stream, mlp_gain[layer_index])
     hidden = jax.nn.gelu(matmul(normed, w_up[layer_index]), approximate=False)
     partial_mlp = matmul(hidden, w_down[layer_index])

time: 515 us -> 541 us (1.050)
  waiting for transfers between devices: 257 us -> 270 us
  other arithmetic: 27 us -> 39 us
    all_gather x0 -> x2, waiting for transfers between devices: none -> 116 us  [save_shapes(): return lax.all_gather(x_part, axis_name=row_axis).sum(axis=0)]
    psum x2 -> x0, waiting for transfers between devices: 102 us -> none  [block_layer(): stream = stream + lax.psum(partial_out, ('col', 'rep'))]
    reduce_sum x0 -> x2, other arithmetic: none -> 12 us  [save_shapes(): return lax.all_gather(x_part, axis_name=row_axis).sum(axis=0)]
  transfers between devices with their start and end apart: 17 -> 17, of which waited for: 12 -> 12; matrix products, arithmetic and copies ran while one was open for 2% -> 1% of each run, Pallas kernels for 0% -> 0%
where the time goes in v1:
time: 541 us; the launch traced here: 536 us
  waiting for transfers between devices  270 us (50%)
  matrix products  164 us (30%)
  other arithmetic  39 us (7%)
  starting transfers between devices  26.2 us (5%)
  local copies, waits for them, and re-layouts  21.6 us (4%)
  between operations  14.3 us (3%)
    all_gather x2, waiting for transfers between devices, save_shapes(): return lax.all_gather(x_part, axis_name=row_axis).sum(axis=0)  116 us
    all_gather x3, waiting for transfers between devices, widen(): return lax.all_gather(slice_cols, ('col', 'rep'), axis=1, tiled=True)  69.2 us
    dot_general x2, matrix products, patch_attention(): jnp.einsum('qhd,khd->hqk', query_projection, key_proj, precision=MATMUL_P...  55.7 us
    reduce_scatter x2, waiting for transfers between devices, block_layer(): lax.psum_scatter(partial_mlp, ('col', 'rep'), scatter_dimension=1, tiled=...  55.4 us
    dot_general x15, matrix products, matmul(): jnp.dot(left, right, precision=MATMUL_PRECISION, preferred_element_type=j...  53.5 us
    dot_general x2, matrix products, patch_attention(): jnp.einsum('hqk,khd->qhd', weights, value_proj, precision=MATMUL_PRECISION)  50.6 us
    unnamed x45, local copies, waits for them, and re-layouts  16.8 us
    all_to_all x1, waiting for transfers between devices, send_blocks(): lax.all_to_all(outgoing, 'tok', split_axis=0, concat_axis=0, tiled=True)  15.6 us
  transfers between devices with their start and end apart: 17, of which 12 were waited for; matrix products, arithmetic and copies ran while one was open for 1% of the time, Pallas kernels for 0%

profile of v1, /device:TPU:1, one launch (start us, length us, event | category | flops | bytes accessed | tf_op | source)
XLA Modules:
  0.0 535.6 jit_solution(18016972037036801910)
XLA Ops:
  9.9 24.3 %all-gather.8.cloned.1.call-done = f32[1024,512]{1,0:T(8,128)} async-done(((f32[1024,128]{1,0:T(8,128)}), f32[1024,512]{1,0:T(8,128)}) %all-gather.8.cloned.1.call-update) | async-done | bytes 2097168 | tf_op jit(solution)/shard_map/all_gather | solution.py:49
  42.0 28.0 %multiply_reduce_fusion.1 = (f32[8,1024]{1,0:T(8,128)S(1)}, f32[8,1024,1024]{1,2,0:T(8,128)S(1)}) fusion(f32[1024,8,16]{0,2,1:T(8,128)S(1)} %fusion.32, f32[1024,8,16]{0,2,1:T(8,128)S(1)} %fusion.30), kind=kOutput, calls=%fused_computation.7 | convolution fusion | flops 1627381760 | bytes 34635776 | tf_op jit(solution)/shard_map/while/body/eval_jaxpr/qhd,khd->hqk/dot_general | solution.py:35
  70.0 5.9 %fusion.4 = f32[8,1024]{1,0:T(8,128)S(1)} fusion(f32[8,1024,1024]{1,2,0:T(8,128)S(1)} %get-tuple-element.80, f32[8,1024]{1,0:T(8,128)S(1)} %get-tuple-element.79), kind=kLoop, calls=%fused_computation.8 | loop fusion | flops 25157632 | bytes 33619968 | tf_op jit(solution)/shard_map/while/body/eval_jaxpr/reduce_sum | solution.py:40
  75.9 5.2 copy-done
  84.4 25.6 %fusion.2 = f32[8,16,1024]{2,1,0:T(8,128)S(1)} fusion(f32[1024,8,16]{0,2,1:T(8,128)} %fusion.34, f32[8,1024,1024]{1,2,0:T(8,128)} %copy-done, f32[8,1024]{1,0:T(8,128)S(1)} %fusion.4, f32[8,1024]{1,0:T(8,128)S(1)} %get-tuple-element.79), kind=kOutput, calls=%fused_computation.4 | convolution fusion | flops 1635778560 | bytes 34668544 | tf_op jit(solution)/shard_map/while/body/eval_jaxpr/hqk,khd->qhd/dot_general | solution.py:41
  110.0 4.2 fusion.299
  114.5 58.2 %all-gather.14.cloned.1.call-done = f32[4096,512]{1,0:T(8,128)} async-done(((f32[1024,512]{1,0:T(8,128)}), f32[4096,512]{1,0:T(8,128)}) %all-gather.14.cloned.1.call-update) | async-done | bytes 8388624 | tf_op jit(solution)/shard_map/all_gather | solution.py:71
  172.7 6.0 %reduce_sum.141 = f32[1024,512]{1,0:T(8,128)} reduce(f32[4,1024,512]{2,1,0:T(8,128)} %bitcast.152, f32[]{:T(128)} %constant.35.clone.1), dimensions={0}, to_apply=%region_5.6 | reduce | flops 1572864 | bytes 10485764 | tf_op jit(solution)/shard_map/reduce_sum | solution.py:71
  186.6 9.3 %fusion.14 = f32[1024,512]{1,0:T(8,128)} fusion(f32[1024,512]{1,0:T(8,128)S(1)} %fusion.143, f32[2,512,512]{2,1,0:T(8,128)S(1)} %copy-done.15), kind=kOutput, calls=%fused_computation.20 | convolution fusion | flops 3254779904 | bytes 5242880 | tf_op jit(solution)/shard_map/dot_general | solution.py:45
  197.6 4.3 all-to-all-start
  201.9 24.8 %reduce-scatter.3.cloned.1.call-done = f32[1024,128]{1,0:T(8,128)} async-done(((f32[1024,512]{1,0:T(8,128)}), f32[1024,128]{1,0:T(8,128)}) %reduce-scatter.3.cloned.1.call-update) | async-done | bytes 524304 | tf_op jit(solution)/shard_map/reduce_scatter | solution.py:77
  229.8 4.3 all-to-all-start.1
  235.4 15.6 %all-to-all-done.1 = f32[4,5,64,128]{3,2,1,0:T(8,128)S(1)} async-done(((f32[4,5,64,128]{3,2,1,0:T(8,128)}), f32[4,5,64,128]{3,2,1,0:T(8,128)S(1)}, u32[]{:S(2)}, u32[]{:S(2)}) %all-to-all-start.1) | async-done | bytes 655392 | tf_op jit(solution)/shard_map/all_to_all | solution.py:105
  253.4 21.6 %all-gather.10.cloned.1.call-done = f32[1024,512]{1,0:T(8,128)} async-done(((f32[1024,128]{1,0:T(8,128)}), f32[1024,512]{1,0:T(8,128)}) %all-gather.10.cloned.1.call-update) | async-done | bytes 2097168 | tf_op jit(solution)/shard_map/all_gather | solution.py:49
  282.8 27.7 %multiply_reduce_fusion = (f32[8,1024]{1,0:T(8,128)S(1)}, f32[8,1024,1024]{1,2,0:T(8,128)S(1)}) fusion(f32[1024,8,16]{0,2,1:T(8,128)S(1)} %fusion.26, f32[1024,8,16]{0,2,1:T(8,128)S(1)} %fusion.24), kind=kOutput, calls=%fused_computation.6 | convolution fusion | flops 1627381760 | bytes 34635776 | tf_op jit(solution)/shard_map/while/body/eval_jaxpr/qhd,khd->hqk/dot_general | solution.py:35
  310.5 5.9 %fusion.5 = f32[8,1024]{1,0:T(8,128)S(1)} fusion(f32[8,1024,1024]{1,2,0:T(8,128)S(1)} %get-tuple-element.82, f32[8,1024]{1,0:T(8,128)S(1)} %get-tuple-element.81), kind=kLoop, calls=%fused_computation.9 | loop fusion | flops 25157632 | bytes 33619968 | tf_op jit(solution)/shard_map/while/body/eval_jaxpr/reduce_sum | solution.py:40
  316.4 5.2 copy-done.1
  324.1 25.0 %fusion = f32[8,16,1024]{2,1,0:T(8,128)S(1)} fusion(f32[1024,8,16]{0,2,1:T(8,128)S(1)} %fusion.28, f32[8,1024,1024]{1,2,0:T(8,128)} %copy-done.1, f32[8,1024]{1,0:T(8,128)S(1)} %fusion.5, f32[8,1024]{1,0:T(8,128)S(1)} %get-tuple-element.81), kind=kOutput, calls=%fused_computation.2 | convolution fusion | flops 1635778560 | bytes 34668544 | tf_op jit(solution)/shard_map/while/body/eval_jaxpr/hqk,khd->qhd/dot_general | solution.py:41
  349.1 4.2 fusion.297
  353.5 58.2 %all-gather.16.cloned.1.call-done = f32[4096,512]{1,0:T(8,128)} async-done(((f32[1024,512]{1,0:T(8,128)}), f32[4096,512]{1,0:T(8,128)}) %all-gather.16.cloned.1.call-update) | async-done | bytes 8388624 | tf_op jit(solution)/shard_map/all_gather | solution.py:71
  411.7 6.0 %reduce_sum.147 = f32[1024,512]{1,0:T(8,128)} reduce(f32[4,1024,512]{2,1,0:T(8,128)} %bitcast.153, f32[]{:T(128)} %constant.35.clone.1), dimensions={0}, to_apply=%region_13.14 | reduce | flops 1572864 | bytes 10485764 | tf_op jit(solution)/shard_map/reduce_sum | solution.py:71
  425.6 9.3 %fusion.18 = f32[1024,512]{1,0:T(8,128)} fusion(f32[1024,512]{1,0:T(8,128)S(1)} %fusion.89, f32[2,512,512]{2,1,0:T(8,128)S(1)} %copy-done.16), kind=kOutput, calls=%fused_computation.23 | convolution fusion | flops 3254779904 | bytes 5242880 | tf_op jit(solution)/shard_map/dot_general | solution.py:45
  435.1 30.7 %reduce-scatter.5.cloned.1.call-done = f32[1024,128]{1,0:T(8,128)} async-done(((f32[1024,512]{1,0:T(8,128)}), f32[1024,128]{1,0:T(8,128)}) %reduce-scatter.5.cloned.1.call-update) | async-done | bytes 524304 | tf_op jit(solution)/shard_map/reduce_scatter | solution.py:77
  468.1 23.3 %all-gather.12.cloned.1.call-done = f32[1024,512]{1,0:T(8,128)} async-done(((f32[1024,128]{1,0:T(8,128)}), f32[1024,512]{1,0:T(8,128)}) %all-gather.12.cloned.1.call-update) | async-done | bytes 2097168 | tf_op jit(solution)/shard_map/all_gather | solution.py:49
  (138 shorter events, 88.6 us)
Async XLA Ops:
  6.5 27.7 %all-gather.8.cloned.1.call-start = ((), (), s32[]{:S(2)}) async-start(), calls=%async_computation.4 | async-start | bytes 2621440 | tf_op jit(solution)/shard_map/all_gather | solution.py:49
  7.3 165.4 %all-gather.14.cloned.1.call-start = ((), (), s32[]{:S(2)}) async-start(), calls=%async_computation.9 | async-start | bytes 10485760 | tf_op jit(solution)/shard_map/all_gather | solution.py:71
  70.0 11.1 %copy-start = (f32[8,1024,1024]{1,2,0:T(8,128)}, f32[8,1024,1024]{1,2,0:T(8,128)S(1)}, u32[]{:S(2)}) copy-start(f32[8,1024,1024]{1,2,0:T(8,128)S(1)} %get-tuple-element.80) | copy-start | bytes 100663296
  114.2 112.4 %reduce-scatter.3.cloned.1.call-start = ((), (), s32[]{:S(2)}) async-start(), calls=%async_computation.5 | async-start | bytes 2621440 | tf_op jit(solution)/shard_map/reduce_scatter | solution.py:77
  180.5 6.0 %copy-start.4 = (f32[1024,512]{1,0:T(8,128)}, f32[1024,512]{1,0:T(8,128)S(1)}, u32[]{:S(2)}) copy-start(f32[1024,512]{1,0:T(8,128)S(1)} %get-tuple-element.31) | copy-start | bytes 6291460
  197.6 32.2 %all-to-all-start = ((f32[4,1,5]{2,1,0:T(1,128)}), f32[4,1,5]{2,1,0:T(1,128)S(1)}, u32[]{:S(2)}, u32[]{:S(2)}) async-start(f32[4,1,5]{2,1,0:T(1,128)} %bitcast.2), calls=%async_computation | async-start | bytes 4096 | tf_op jit(solution)/shard_map/all_to_all | solution.py:106
  229.8 21.2 %all-to-all-start.1 = ((f32[4,5,64,128]{3,2,1,0:T(8,128)}), f32[4,5,64,128]{3,2,1,0:T(8,128)S(1)}, u32[]{:S(2)}, u32[]{:S(2)}) async-start(f32[4,5,64,128]{3,2,1,0:T(8,128)} %copy.48), calls=%async_computation.2 | async-start | bytes 1310720 | tf_op jit(solution)/shard_map/all_to_all | solution.py:105
  234.1 40.9 %all-gather.10.cloned.1.call-start = ((), (), s32[]{:S(2)}) async-start(), calls=%async_computation.6 | async-start | bytes 2621440 | tf_op jit(solution)/shard_map/all_gather | solution.py:49
  252.8 159.0 %all-gather.16.cloned.1.call-start = ((), (), s32[]{:S(2)}) async-start(), calls=%async_computation.10 | async-start | bytes 10485760 | tf_op jit(solution)/shard_map/all_gather | solution.py:71
  310.5 11.1 %copy-start.1 = (f32[8,1024,1024]{1,2,0:T(8,128)}, f32[8,1024,1024]{1,2,0:T(8,128)S(1)}, u32[]{:S(2)}) copy-start(f32[8,1024,1024]{1,2,0:T(8,128)S(1)} %get-tuple-element.82) | copy-start | bytes 100663296
  353.3 112.4 %reduce-scatter.5.cloned.1.call-start = ((), (), s32[]{:S(2)}) async-start(), calls=%async_computation.7 | async-start | bytes 2621440 | tf_op jit(solution)/shard_map/reduce_scatter | solution.py:77
  435.0 33.0 %copy-start.9 = (f32[2,3,3,512]{3,0,2,1:T(2,128)S(1)}, f32[2,3,3,512]{3,0,2,1:T(2,128)}, u32[]{:S(2)}) copy-start(f32[2,3,3,512]{3,0,2,1:T(2,128)} %param.23) | copy-start | bytes 110596
  435.0 56.4 %copy-start.13 = (s32[1024]{0:T(1024)S(1)}, s32[1024]{0:T(1024)}, u32[]{:S(2)}) copy-start(s32[1024]{0:T(1024)} %param.22) | copy-start | bytes 12292
  435.0 56.4 %all-gather.12.cloned.1.call-start = ((), (), s32[]{:S(2)}) async-start(), calls=%async_computation.8 | async-start | bytes 2621440 | tf_op jit(solution)/shard_map/all_gather | solution.py:49
  467.8 38.7 %copy-start.12 = (f32[2,512]{1,0:T(2,128)S(1)}, f32[2,512]{1,0:T(2,128)}, u32[]{:S(2)}) copy-start(f32[2,512]{1,0:T(2,128)} %param.25) | copy-start | bytes 12292
  491.4 18.4 %copy-start.14 = (f32[2,512,1024]{2,1,0:T(8,128)S(1)}, f32[2,512,1024]{2,1,0:T(8,128)}, u32[]{:S(2)}) copy-start(f32[2,512,1024]{2,1,0:T(8,128)} %param.24) | copy-start | bytes 12582916
  494.2 5.2 collective-permute-start
  497.5 5.2 collective-permute-start.1
  502.8 3.7 collective-permute-start.2
  504.9 4.5 collective-permute-start.3
  511.4 5.3 collective-permute-start.4
  514.7 5.2 collective-permute-start.5
  520.0 2.7 collective-permute-start.6
  521.4 4.5 collective-permute-start.7
  (12 other events, 34.1 us)
Sparse Core Ops, SparseCore 0:
  8.9 25.2 all-gather.7
  114.4 58.2 all-gather.13
  196.1 30.5 reduce-scatter.2
  252.9 22.0 all-gather.9
  353.4 58.2 all-gather.15
  435.1 30.5 reduce-scatter.4
  467.9 23.3 all-gather.11
